TPU v7x, 256 devices: a whole 4x4x8 slice. The times are simulated.
256 devices in a mesh: group: 16 (over z, core), helper: 16 (over y, x).
Axes of the slice: x: 4, y: 4, z: 8, core: 2. Of those that a mesh axis runs over, the one named last changes fastest.
Arguments:
- candidates: bfloat16 [2048, 128, 1024], P(('group', 'helper')), may hold values from -36 to 36
- block_user: int32 [2048], P(('group', 'helper')), may hold values from 0 to 15, as said below
- live_rows: int32 [2048], P(('group', 'helper')), may hold values from 1 to 128
- prefix_keys: bfloat16 [256, 256, 1024], P(('group', 'helper')), may hold values from -6 to 6
- prefix_values: bfloat16 [256, 256, 1024], P(('group', 'helper')), may hold values from -6 to 6
- w_proj: bfloat16 [1024, 4096], P(('group', 'helper')), may hold values from -0.1875 to 0.1875
- w_out: bfloat16 [1024, 1024], P(('group', 'helper')), may hold values from -0.1875 to 0.1875
- gain_in: float32 [1024], replicated, may hold values from 0.1 to 1.9
- gain_mid: float32 [1024], replicated, may hold values from 0.1 to 1.9
- score_vec: float32 [1024], replicated, may hold values from -0.1875 to 0.1875
Outputs:
- embeddings: bfloat16 [2048, 128, 1024], P(('group', 'helper'))
- scores: float32 [2048, 128], P(('group', 'helper'))
Inputs may be any that keep to these rules, and one draw needn't show every extreme that they name: `block_user`: the 8 blocks of one device name different users; in every group some user is named by a block of every device of the group.
All inputs are finite; a program needn't handle non-finite values.
Results may differ from a plain program's by a relative error of at most 0.0045.
Values may be sent and summed in bfloat16 or wider, within the bound.
A program may use at most 128 MiB of HBM per device.

v0:
```python
import jax
import jax.numpy as jnp
from jax import lax
from jax.sharding import PartitionSpec as P

HEADS = 8


epsilon = 1e-05


def side_by_side(arrays, axis, dim, along):
    widths = [a.shape[along] for a in arrays]
    both = jnp.concatenate(arrays, axis=along)
    filled = lax.all_gather(both, axis, axis=dim, tiled=True)
    return tuple(jnp.split(filled, [sum(widths[:k]) for k in range(1, len(widths))], axis=along))


def exchange_in_groups(array, axis, split_dim, concat_dim, work, item_dim, out_dim):
    items = jax.tree.leaves(array)[0].shape[item_dim]
    count = 2 if items % 2 == 0 else 1
    done = []
    for k in range(count):
        group = jax.tree.map(
            lambda a: lax.slice_in_dim(
                a, k * (items // count), (k + 1) * (items // count), axis=item_dim
            ),
            array,
        )
        done.append(
            work(
                lax.all_to_all(
                    group, axis, split_axis=split_dim, concat_axis=concat_dim, tiled=True
                )
            )
        )
    return jax.tree.map(lambda *parts: jnp.concatenate(parts, axis=out_dim), *done)


def layer_norm(values, gain):
    average = jnp.mean(values, axis=-1, keepdims=True)
    centred = values - average
    spread = jnp.mean(centred * centred, axis=-1, keepdims=True)
    return centred * lax.rsqrt(spread + epsilon) * gain


def shards(
    candidates,
    block_user,
    live_rows,
    prefix_keys,
    prefix_values,
    w_proj,
    w_out,
    gain_in,
    gain_mid,
    score_vec,
):
    helpers = lax.axis_size("helper")
    blocks, rows_block, features = candidates.shape
    head_dim = features // HEADS
    score_scale = head_dim ** (-0.5)
    proj_part, out_part = side_by_side((w_proj, w_out), "helper", 0, 1)
    proj_full, out_full = side_by_side((proj_part, out_part), "group", 0, 1)
    cand_rows = candidates.reshape(blocks * rows_block, features).astype(jnp.float32)
    normed = layer_norm(cand_rows, gain_in).astype(jnp.bfloat16)
    projected = jax.nn.silu(jnp.dot(normed, proj_full, preferred_element_type=jnp.float32))
    gate_portion = projected[:, :features]
    value_part = projected[:, features : 2 * features]
    query_portion = projected[:, 2 * features : 3 * features]
    key_part = projected[:, 3 * features :]
    query_bf = lax.optimization_barrier(query_portion.astype(jnp.bfloat16))
    query_heads = query_bf.astype(jnp.float32).reshape(-1, HEADS, head_dim)
    own_weight = jax.nn.silu(
        score_scale * jnp.sum(query_heads * key_part.reshape(-1, HEADS, head_dim), axis=-1)
    )
    own_term = (own_weight[..., None] * value_part.reshape(-1, HEADS, head_dim)).reshape(
        -1, features
    )
    onehot = (block_user[None, :] == jnp.arange(helpers, dtype=jnp.int32)[:, None]).astype(
        jnp.bfloat16
    )
    outgoing = jnp.dot(
        onehot, query_bf.reshape(blocks, rows_block * features), preferred_element_type=jnp.float32
    )
    outgoing = outgoing.astype(jnp.bfloat16).reshape(helpers, rows_block, features)
    per_head_keys = prefix_keys[0].reshape(-1, HEADS, head_dim)
    per_head_values = prefix_values[0].reshape(-1, HEADS, head_dim)

    def attended_row_set(query_tile_group):
        raw_scores = jnp.einsum(
            "ocy,qcy->coq", query_tile_group, per_head_keys, preferred_element_type=jnp.float32
        )
        weight_brainfloat = jax.nn.silu(score_scale * raw_scores).astype(jnp.bfloat16)
        return jnp.einsum(
            "txw,wta->xta", weight_brainfloat, per_head_values, preferred_element_type=jnp.float32
        ).astype(jnp.bfloat16)

    def attend(arrived):
        arrived_shape = arrived.shape
        count_rows = arrived_shape[0] * arrived_shape[1]
        flat_query = arrived.reshape(count_rows, HEADS, head_dim)
        if count_rows > 512 and count_rows % 512 == 0:
            mixed_heads = lax.map(
                attended_row_set, flat_query.reshape(count_rows // 512, 512, HEADS, head_dim)
            )
        else:
            mixed_heads = attended_row_set(flat_query)
        return lax.all_to_all(
            mixed_heads.reshape(arrived_shape), "helper", split_axis=0, concat_axis=0, tiled=True
        )

    returned = exchange_in_groups(outgoing, "helper", 0, 0, attend, 1, 1)
    prefix_mix = jnp.einsum(
        "jb,jf->bf",
        onehot,
        returned.reshape(helpers, rows_block * features),
        preferred_element_type=jnp.float32,
    )
    mixed = prefix_mix.reshape(-1, features) + own_term
    gated = (layer_norm(mixed, gain_mid) * gate_portion).astype(jnp.bfloat16)
    updated = cand_rows + jnp.dot(gated, out_full, preferred_element_type=jnp.float32)
    embeddings = updated.astype(jnp.bfloat16).reshape(blocks, rows_block, features)
    row_scores = jnp.sum(layer_norm(updated, 1.0) * score_vec, axis=-1).reshape(blocks, rows_block)
    live_mask = jnp.arange(rows_block, dtype=jnp.int32)[None, :] < live_rows[:, None]
    scores = jnp.where(live_mask, row_scores, jnp.zeros_like(row_scores))
    return (embeddings, scores)


def solution(mesh):
    placed = (
        P(("group", "helper"), None, None),
        P(("group", "helper")),
        P(("group", "helper")),
        P(("group", "helper"), None, None),
        P(("group", "helper"), None, None),
        P(("group", "helper"), None),
        P(("group", "helper"), None),
        P(),
        P(),
        P(),
    )
    return jax.shard_map(
        shards,
        mesh=mesh,
        in_specs=placed,
        out_specs=(P(("group", "helper"), None, None), P(("group", "helper"), None)),
        check_vma=False,
    )
```

profile of v0, /device:TPU:1, one launch (start us, length us, event | category | flops | bytes accessed | tf_op | source)
XLA Modules:
  0.0 305.1 jit_solution(9503130203791252425)
XLA Ops:
  8.2 20.1 %all-gather = bf16[16,4,5120]{2,1,0:T(4,128)(2,1)S(1)} all-gather(bf16[1,4,5120]{2,1,0:T(4,128)(2,1)S(1)} %maximum_bitcast_fusion), channel_id=1, replica_groups=mesh['group'=16,'helper'=16] {'helper'}, dimensions={0}, use_global_device_ids=true | all-gather | bytes 696320 | tf_op jit(solution)/shard_map/all_gather | solution.py:15
  29.3 1.9 convert_reduce_fusion
  32.0 2.0 fusion.19
  34.0 67.6 %all-gather.3.cloned.1.call-done = bf16[1024,5120]{1,0:T(8,128)(2,1)} async-done(((bf16[64,5120]{1,0:T(8,128)(2,1)}), bf16[1024,5120]{1,0:T(8,128)(2,1)}) %all-gather.3.cloned.1.call-update) | async-done | bytes 10485776 | tf_op jit(solution)/shard_map/all_gather | solution.py:15
  101.6 13.2 %divide_multiply_fusion = f32[1024,4096]{1,0:T(8,128)S(1)} fusion(bf16[1024,1024]{1,0:T(8,128)(2,1)} %fusion.19, bf16[1024,5120]{1,0:T(8,128)(2,1)} %all-gather.3.cloned.1.call-done), kind=kOutput, calls=%fused_computation.19 | convolution fusion | flops 8606711808 | bytes 27262976 | tf_op jit(solution)/shard_map/dot_general | solution.py:67
  114.8 5.7 %copy-done.5 = f32[1024,4096]{1,0:T(8,128)} copy-done((f32[1024,4096]{1,0:T(8,128)}, f32[1024,4096]{1,0:T(8,128)S(1)}, u32[]{:S(2)}) %copy-start.5) | copy-done | bytes 16777240
  120.8 2.3 reshape.106
  123.1 2.8 convolution_convert_fusion
  125.9 2.3 copy.61
  128.3 2.4 fusion.38
  130.7 6.7 %all-to-all-start = ((bf16[16,64,1024]{2,1,0:T(8,128)(2,1)}), bf16[16,64,1024]{2,1,0:T(8,128)(2,1)S(1)}, u32[]{:S(2)}, u32[]{:S(2)}) async-start(bf16[16,64,1024]{2,1,0:T(8,128)(2,1)} %get-tuple-element.122), calls=%async_computation | async-start | bytes 4194304 | tf_op jit(solution)/shard_map/all_to_all | solution.py:32
  140.1 29.9 %all-to-all-done = bf16[16,64,1024]{2,1,0:T(8,128)(2,1)S(1)} async-done(((bf16[16,64,1024]{2,1,0:T(8,128)(2,1)}), bf16[16,64,1024]{2,1,0:T(8,128)(2,1)S(1)}, u32[]{:S(2)}, u32[]{:S(2)}) %all-to-all-start) | async-done | bytes 2097184 | tf_op jit(solution)/shard_map/all_to_all | solution.py:32
  170.0 4.4 %all-to-all-start.2 = ((bf16[16,64,1024]{2,1,0:T(8,128)(2,1)}), bf16[16,64,1024]{2,1,0:T(8,128)(2,1)}, u32[]{:S(2)}, u32[]{:S(2)}) async-start(bf16[16,64,1024]{2,1,0:T(8,128)(2,1)} %get-tuple-element.123), calls=%async_computation.2 | async-start | bytes 4194304 | tf_op jit(solution)/shard_map/all_to_all | solution.py:32
  174.4 2.0 copy.62
  176.4 1.6 broadcast.103.clone2.1
  178.0 9.7 %while.20 = (s32[]{:T(128)}, bf16[2,512,8,128]{3,2,1,0:T(8,128)(2,1)}, bf16[2,512,8,128]{3,2,1,0:T(8,128)(2,1)}, bf16[256,8,128]{2,0,1:T(8,128)(2,1)S(1)}, bf16[256,8,128]{2,0,1:T(8,128)(2,1)S(1)}, /*index=5*/s32[]{:T(128)}) while((s32[]{:T(128)}, bf16[2,512,8,128]{3,2,1,0:T(8,128)(2,1)}, bf16[2,512,8,128]{3,2,1,0:T(8,128)(2,1)}, ...), condition=%wide.region_3.4_spmd, body=%wide.region_2.3_spmd.sunk | while | flops 543686656 | bytes 7340617 | solution.py:104
  178.0 1.3 constant_dynamic-slice_fusion.4
  179.3 1.9 fusion.55
  181.2 1.7 copy_dynamic-update-slice_fusion.4
  182.8 1.3 constant_dynamic-slice_fusion.4
  184.1 1.9 fusion.55
  186.0 1.7 copy_dynamic-update-slice_fusion.4
  187.7 4.2 %reshape.108 = bf16[16,64,1024]{2,1,0:T(8,128)(2,1)} reshape(bf16[2,512,8,128]{3,2,1,0:T(8,128)(2,1)} %get-tuple-element.56) | data formatting | bytes 4194304 | tf_op jit(solution)/shard_map/reshape | solution.py:110
  191.9 12.1 %all-to-all-done.2 = bf16[16,64,1024]{2,1,0:T(8,128)(2,1)} async-done(((bf16[16,64,1024]{2,1,0:T(8,128)(2,1)}), bf16[16,64,1024]{2,1,0:T(8,128)(2,1)}, u32[]{:S(2)}, u32[]{:S(2)}) %all-to-all-start.2) | async-done | bytes 2097184 | tf_op jit(solution)/shard_map/all_to_all | solution.py:32
  204.0 4.9 %all-to-all-start.1 = ((bf16[16,64,1024]{2,1,0:T(8,128)(2,1)}), bf16[16,64,1024]{2,1,0:T(8,128)(2,1)}, u32[]{:S(2)}, u32[]{:S(2)}) async-start(bf16[16,64,1024]{2,1,0:T(8,128)(2,1)} %reshape.108), calls=%async_computation.1 | async-start | bytes 4194304 | tf_op jit(solution)/shard_map/all_to_all | solution.py:109
  208.9 3.6 %copy.63 = bf16[128,8,8,128]{3,2,1,0:T(8,128)(2,1)} copy(bf16[128,8,8,128]{3,1,2,0:T(8,128)(2,1)} %bitcast.24) | data formatting | bytes 4194304
  212.5 1.6 broadcast.103.clone2
  214.1 9.7 %while.21 = (s32[]{:T(128)}, bf16[2,512,8,128]{3,2,1,0:T(8,128)(2,1)}, bf16[2,512,8,128]{3,2,1,0:T(8,128)(2,1)}, bf16[256,8,128]{2,0,1:T(8,128)(2,1)S(1)}, bf16[256,8,128]{2,0,1:T(8,128)(2,1)S(1)}, /*index=5*/s32[]{:T(128)}) while((s32[]{:T(128)}, bf16[2,512,8,128]{3,2,1,0:T(8,128)(2,1)}, bf16[2,512,8,128]{3,2,1,0:T(8,128)(2,1)}, ...), condition=%wide.region_5.6_spmd, body=%wide.region_4.5_spmd.sunk | while | flops 543686656 | bytes 7340617 | solution.py:104
  214.1 1.3 constant_dynamic-slice_fusion.5
  215.4 1.9 fusion.58
  217.3 1.7 copy_dynamic-update-slice_fusion.5
  218.9 1.3 constant_dynamic-slice_fusion.5
  220.2 1.9 fusion.58
  222.1 1.7 copy_dynamic-update-slice_fusion.5
  223.8 4.3 %reshape.109 = bf16[16,64,1024]{2,1,0:T(8,128)(2,1)} reshape(bf16[2,512,8,128]{3,2,1,0:T(8,128)(2,1)} %get-tuple-element.57) | data formatting | bytes 4194304 | tf_op jit(solution)/shard_map/reshape | solution.py:110
  228.1 8.2 %all-to-all-done.1 = bf16[16,64,1024]{2,1,0:T(8,128)(2,1)} async-done(((bf16[16,64,1024]{2,1,0:T(8,128)(2,1)}), bf16[16,64,1024]{2,1,0:T(8,128)(2,1)}, u32[]{:S(2)}, u32[]{:S(2)}) %all-to-all-start.1) | async-done | bytes 2097184 | tf_op jit(solution)/shard_map/all_to_all | solution.py:109
  236.4 6.4 %all-to-all-start.3 = ((bf16[16,64,1024]{2,1,0:T(8,128)(2,1)}), bf16[16,64,1024]{2,1,0:T(8,128)(2,1)}, u32[]{:S(2)}, u32[]{:S(2)}) async-start(bf16[16,64,1024]{2,1,0:T(8,128)(2,1)} %reshape.109), calls=%async_computation.3 | async-start | bytes 4194304 | tf_op jit(solution)/shard_map/all_to_all | solution.py:109
  242.7 2.9 fusion.14
  245.6 3.1 %copy.65 = f32[128,8,8,128]{3,2,1,0:T(8,128)} copy(f32[128,8,8,128]{3,1,2,0:T(8,128)S(1)} %fusion.14) | data formatting | bytes 8388608
  248.7 3.4 %reduce_sum.74 = f32[1024,8]{1,0:T(8,128)S(1)} reduce(f32[1024,8,128]{2,1,0:T(8,128)} %bitcast.87, f32[]{:T(128)} %constant.44.clone.1), dimensions={2}, to_apply=%region_6.7 | reduce | flops 1040384 | bytes 4227076 | tf_op jit(solution)/shard_map/reduce_sum | solution.py:75
  252.4 16.9 %all-to-all-done.3 = bf16[16,64,1024]{2,1,0:T(8,128)(2,1)} async-done(((bf16[16,64,1024]{2,1,0:T(8,128)(2,1)}), bf16[16,64,1024]{2,1,0:T(8,128)(2,1)}, u32[]{:S(2)}, u32[]{:S(2)}) %all-to-all-start.3) | async-done | bytes 2097184 | tf_op jit(solution)/shard_map/all_to_all | solution.py:109
  269.3 2.8 pad_maximum_fusion
  272.2 2.3 copy.64
  274.5 2.6 fusion.32
  277.1 4.9 %reshape.111 = f32[1024,1024]{1,0:T(8,128)} reshape(f32[8,131072]{1,0:T(8,128)} %fusion.32) | data formatting | bytes 8388608 | tf_op jit(solution)/shard_map/reshape | solution.py:120
  284.2 3.3 %fusion.36 = (f32[1024]{0:T(1024)S(1)}, f32[1024,1024]{1,0:T(8,128)S(1)}) fusion(f32[1024,1024]{1,0:T(8,128)S(1)} %copy-done.4, f32[1024,4096]{1,0:T(8,128)} %copy-done.5, f32[128,8,8,128]{3,2,1,0:T(8,128)S(1)} %bitcast.85), kind=kLoop, calls=%fused_computation.62 | loop fusion | flops 3144704 | bytes 16781312 | tf_op jit(solution)/shard_map/reduce_sum | solution.py:41
  289.1 5.4 %fusion.39 = (f32[1024]{0:T(1024)S(1)}, f32[1024,1024]{1,0:T(8,128)S(1)}) fusion(bf16[1024,5120]{1,0:T(8,128)(2,1)} %all-gather.3.cloned.1.call-done, f32[1024,4096]{1,0:T(8,128)} %copy-done.5, f32[1024,1024]{1,0:T(8,128)S(1)} %get-tuple-element.119, f32[1024]{0:T(1024)S(1)} %copy-done.12, f32[1024]{0:T(1024)S(1)} %add_rsqrt_fusion.1, ...), kind=kOutput, calls=%fused_computation.64 | convolution fusion | flops 2155871232 | bytes 16793600 | tf_op jit(solution)/shard_map/dot_general | solution.py:122
  295.2 2.3 multiply_reduce_fusion
  (48 shorter events, 11.2 us)
Async XLA Ops:
  7.2 24.1 %copy-start = (bf16[8,128,1024]{2,1,0:T(8,128)(2,1)S(1)}, bf16[8,128,1024]{2,1,0:T(8,128)(2,1)}, u32[]{:S(2)}) copy-start(bf16[8,128,1024]{2,1,0:T(8,128)(2,1)} %param.14) | copy-start | bytes 6291460
  7.2 24.8 %copy-start.8 = (f32[1024]{0:T(1024)S(1)}, f32[1024]{0:T(1024)}, u32[]{:S(2)}) copy-start(f32[1024]{0:T(1024)} %param.21) | copy-start | bytes 12292
  7.2 94.4 %all-gather.3.cloned.1.call-start = ((), (), s32[]{:S(2)}) async-start(), calls=%async_computation.4 | async-start | bytes 11141120 | tf_op jit(solution)/shard_map/all_gather | solution.py:15
  114.8 5.7 %copy-start.5 = (f32[1024,4096]{1,0:T(8,128)}, f32[1024,4096]{1,0:T(8,128)S(1)}, u32[]{:S(2)}) copy-start(f32[1024,4096]{1,0:T(8,128)S(1)} %divide_multiply_fusion) | copy-start | bytes 50331652
  120.5 2.6 copy-start.10
  120.8 5.1 %copy-start.2 = (bf16[1024,1024]{1,0:T(8,128)(2,1)}, bf16[1024,1024]{1,0:T(8,128)(2,1)S(1)}, u32[]{:S(2)}) copy-start(bf16[1024,1024]{1,0:T(8,128)(2,1)S(1)} %slice.43) | copy-start | bytes 6291460
  130.7 6.7 %copy-start.6 = (bf16[1,256,1024]{2,1,0:T(8,128)(2,1)S(1)}, bf16[1,256,1024]{2,1,0:T(8,128)(2,1)}, u32[]{:S(2)}) copy-start(bf16[1,256,1024]{2,1,0:T(8,128)(2,1)} %param.17) | copy-start | bytes 1572868
  130.7 39.3 %all-to-all-start = ((bf16[16,64,1024]{2,1,0:T(8,128)(2,1)}), bf16[16,64,1024]{2,1,0:T(8,128)(2,1)S(1)}, u32[]{:S(2)}, u32[]{:S(2)}) async-start(bf16[16,64,1024]{2,1,0:T(8,128)(2,1)} %get-tuple-element.122), calls=%async_computation | async-start | bytes 4194304 | tf_op jit(solution)/shard_map/all_to_all | solution.py:32
  170.0 34.0 %all-to-all-start.2 = ((bf16[16,64,1024]{2,1,0:T(8,128)(2,1)}), bf16[16,64,1024]{2,1,0:T(8,128)(2,1)}, u32[]{:S(2)}, u32[]{:S(2)}) async-start(bf16[16,64,1024]{2,1,0:T(8,128)(2,1)} %get-tuple-element.123), calls=%async_computation.2 | async-start | bytes 4194304 | tf_op jit(solution)/shard_map/all_to_all | solution.py:32
  174.4 3.6 %copy-start.7 = (bf16[256,8,128]{2,0,1:T(8,128)(2,1)S(1)}, bf16[256,8,128]{2,0,1:T(8,128)(2,1)}, u32[]{:S(2)}) copy-start(bf16[256,8,128]{2,0,1:T(8,128)(2,1)} %copy.47) | copy-start | bytes 1572868
  204.0 32.3 %all-to-all-start.1 = ((bf16[16,64,1024]{2,1,0:T(8,128)(2,1)}), bf16[16,64,1024]{2,1,0:T(8,128)(2,1)}, u32[]{:S(2)}, u32[]{:S(2)}) async-start(bf16[16,64,1024]{2,1,0:T(8,128)(2,1)} %reshape.108), calls=%async_computation.1 | async-start | bytes 4194304 | tf_op jit(solution)/shard_map/all_to_all | solution.py:109
  223.8 19.0 %copy-start.3 = (bf16[1024,1024]{1,0:T(8,128)(2,1)S(1)}, bf16[1024,1024]{1,0:T(8,128)(2,1)}, u32[]{:S(2)}) copy-start(bf16[1024,1024]{1,0:T(8,128)(2,1)} %copy-done.2) | copy-start | bytes 6291460
  236.4 33.0 %all-to-all-start.3 = ((bf16[16,64,1024]{2,1,0:T(8,128)(2,1)}), bf16[16,64,1024]{2,1,0:T(8,128)(2,1)}, u32[]{:S(2)}, u32[]{:S(2)}) async-start(bf16[16,64,1024]{2,1,0:T(8,128)(2,1)} %reshape.109), calls=%async_computation.3 | async-start | bytes 4194304 | tf_op jit(solution)/shard_map/all_to_all | solution.py:109
  282.0 2.2 copy-start.4
  287.5 1.6 copy-start.1
  287.5 1.6 copy-start.12
  294.6 0.7 copy-start.9
  295.1 2.5 copy-start.11
Sparse Core Ops, SparseCore 0:
  29.4 72.1 all-gather.2
where the time goes:
time: 308 us; the launch traced here: 305 us
  waiting for transfers between devices  135 us (44%)
  local copies, waits for them, and re-layouts  59.7 us (19%)
  matrix products  31.6 us (10%)
  starting transfers between devices  22.4 us (7%)
  other arithmetic  22.1 us (7%)
  blocking collectives  20.1 us (7%)
  between operations  14.3 us (5%)
    all_gather x1, waiting for transfers between devices, side_by_side(): filled = lax.all_gather(both, axis, axis=dim, tiled=True)  67.6 us
    all_to_all x2, waiting for transfers between devices, exchange_in_groups(): lax.all_to_all(group, axis, split_axis=split_dim, concat_axis=concat_dim,...  42 us
    all_to_all x2, waiting for transfers between devices, attend(): lax.all_to_all(mixed_heads.reshape(arrived_shape), 'helper', split_axis=0...  25.1 us
    unnamed x34, local copies, waits for them, and re-layouts  23.6 us
    all_gather x1, blocking collectives, side_by_side(): filled = lax.all_gather(both, axis, axis=dim, tiled=True)  20.1 us
    dot_general x1, matrix products, shards(): jnp.dot(normed, proj_full, preferred_element_type=jnp.float32)  13.2 us
    all_to_all x2, starting transfers between devices, attend(): lax.all_to_all(mixed_heads.reshape(arrived_shape), 'helper', split_axis=0...  11.2 us
    all_to_all x2, starting transfers between devices, exchange_in_groups(): lax.all_to_all(group, axis, split_axis=split_dim, concat_axis=concat_dim,...  11.1 us
  transfers between devices with their start and end apart: 5, of which 5 were waited for; matrix products, arithmetic and copies ran while one was open for 18% of the time, Pallas kernels for 0%

commit v1 on v0

v1 whole, which is shorter than its diff:
```python
import functools

import jax
import jax.numpy as jnp
from jax import lax
from jax.experimental import pallas as pl
from jax.experimental.pallas import tpu as pltpu
from jax.sharding import PartitionSpec as P

MESH = pl.DeviceIdType.MESH
HEADS = 8
EPS = 1e-05
CHUNKS = 4
HOLD = ((0, 0), (0, 1), (1, 0), (0, 2), (2, 0), (2, 3))
PARENT = (None, 0, 0, 1, 2, 4)
LEVELS = ((1, 2), (3, 4), (5,))


def split_others():
    ways = ((0, 1), (0, 3), (1, 0), (3, 0))
    groups = {way: [] for way in ways}
    rest = []
    for y in range(4):
        for x in range(4):
            if (y, x) not in HOLD:
                near = {w: (((y + w[0]) % 4), (x + w[1]) % 4) for w in ways}
                rest.append([(w, HOLD.index(n)) for w, n in near.items() if n in HOLD])
    for options in sorted(rest, key=len):
        way, held = min(options, key=lambda o: len(groups[o[0]]))
        groups[way].append(held)
    return tuple((way, tuple(held)) for way, held in groups.items() if held)


GROUPS = split_others()
STARTS = tuple(sum(len(h) for _, h in GROUPS[:k]) for k in range(len(GROUPS)))
SENT = tuple((way, held) for way, helds in GROUPS for held in helds)
HERE = len(HOLD)
PAIRS = HERE + len(SENT)


def turn(offset, c):
    dy, dx = offset
    even, odd = (1 - c % 2) * (1 - c), (c % 2) * (2 - c)
    return even * dy + odd * dx, even * dx - odd * dy


def silu(v):
    half = 0.5 * v
    return half + half * jnp.tanh(half)


def centred(v):
    v = v - jnp.mean(v, axis=-1, keepdims=True)
    return v * lax.rsqrt(jnp.mean(v * v, axis=-1, keepdims=True) + EPS)


def kernel(
    cand, users, live, keys, values, w_proj, w_out, gain_in, gain_mid, score_vec,
    emb, scores,
    xb, normed, wraw, wfull, kv, q, own, gate, qs, qr, res, mix, block_of, place_of,
    loc, w1s, w1r, zs, zr, ps, pr, ks, kr, qss, qrs, rss, rrs,
):
    g, h = lax.axis_index("group"), lax.axis_index("helper")
    z, core = g // 2, g % 2
    y, x = h // 4, h % 4
    blocks, rows, width = xb.shape
    part = wraw.shape[2] // 5
    cols = width // CHUNKS
    alpha = (width // HEADS) ** -0.5

    def plane(offset):
        return lax.rem(y + offset[0] + 8, 4) * 4 + lax.rem(x + offset[1] + 8, 4)

    def along(step):
        return lax.rem(z + step + 8, 8)

    local = [
        pltpu.make_async_copy(w_proj, wraw.at[h, :, pl.ds(0, 4 * part)], loc.at[0]),
        pltpu.make_async_copy(w_out, wraw.at[h, :, pl.ds(4 * part, part)], loc.at[1]),
        pltpu.make_async_copy(cand, xb, loc.at[2]),
    ]
    for c in range(CHUNKS):
        for k, src in enumerate((keys, values)):
            local.append(
                pltpu.make_async_copy(
                    src.at[0, :, pl.ds(c * cols, cols)],
                    kv.at[c, 0, pl.ds(k * 256, 256)],
                    loc.at[3 + 2 * c + k],
                )
            )
    for copy in local:
        copy.start()

    barrier = pltpu.get_barrier_semaphore()
    peers = [(g, lax.rem(h + k, 16)) for k in range(1, 16)]
    peers += [(2 * along(1) + core, h), (2 * along(-1) + core, h), (2 * z + 1 - core, h)]
    for peer in peers:
        pl.semaphore_signal(barrier, inc=1, device_id=peer, device_id_type=MESH)
    pl.semaphore_wait(barrier, len(peers))

    sent = []

    def send(src, dst, s, r, device):
        copy = pltpu.make_async_remote_copy(
            src_ref=src, dst_ref=dst, send_sem=s, recv_sem=r, device_id=device, device_id_type=MESH
        )
        copy.start()
        return copy

    local[0].wait()
    local[1].wait()

    def w1(k, at):
        return pltpu.make_async_remote_copy(
            src_ref=wraw.at[at], dst_ref=wraw.at[at], send_sem=w1s.at[k], recv_sem=w1r.at[k],
            device_id=(g, lax.rem(h + k, 16)), device_id_type=MESH,
        )

    for k in range(1, 16):
        copy = w1(k, h)
        copy.start()
        sent.append(copy)

    def kv_send(c, child):
        parent = PARENT[child]
        a, b = HOLD[parent], HOLD[child]
        step = turn((b[0] - a[0], b[1] - a[1]), c)
        step = tuple((s + 2) % 4 - 2 if s not in (2, -2) else s for s in step)
        return pltpu.make_async_remote_copy(
            src_ref=kv.at[c, parent], dst_ref=kv.at[c, child], send_sem=ks.at[c, child],
            recv_sem=kr.at[c, child], device_id=(g, plane(step)), device_id_type=MESH,
        )

    def kv_level(level, after):
        for c in range(CHUNKS):
            if level == 0:
                local[3 + 2 * c].wait()
                local[4 + 2 * c].wait()
            for child in LEVELS[level]:
                if PARENT[child]:
                    kv_send(c, PARENT[child]).wait_recv()
                copy = kv_send(c, child)
                copy.start()
                sent.append(copy)

    kv_level(0, None)

    for u in range(16):
        found = jnp.int32(0)
        for b in range(blocks):
            found = jnp.where(users[b] == u, jnp.int32(b), found)
        block_of[u] = found

    def user_of(c, p):
        if p < HERE:
            dy, dx = turn(HOLD[p], c)
            return plane((-dy, -dx))
        way, held = SENT[p - HERE]
        dy, dx = turn((way[0] - HOLD[held][0], way[1] - HOLD[held][1]), c)
        return plane((dy, dx))

    for c in range(CHUNKS):
        for p in range(PAIRS):
            place_of[c * 16 + user_of(c, p)] = jnp.int32(p)

    local[2].wait()

    @pl.loop(0, blocks)
    def _(b):
        v = centred(xb[b].astype(jnp.float32)) * gain_in[...]
        normed[pl.ds(pl.multiple_of(b * rows, rows), rows), :] = v.astype(jnp.bfloat16)

    def slab(at, of_core):
        return pl.ds(pl.multiple_of((2 * at + of_core) * 64, 64), 64)

    def z_copy(j, t, unit, way, at):
        ref = wfull.at[j, slab(at, core), pl.ds(unit * (part // 2), part // 2)]
        where = (t * 2 + unit) * 2 + way
        return pltpu.make_async_remote_copy(
            src_ref=ref, dst_ref=ref, send_sem=zs.at[j, where], recv_sem=zr.at[j, where],
            device_id=(2 * along(1 - 2 * way) + core, h), device_id_type=MESH,
        )

    def p_copy(j, n, at, of_core):
        ref = wfull.at[j, slab(at, of_core)]
        return pltpu.make_async_remote_copy(
            src_ref=ref, dst_ref=ref, send_sem=ps.at[j, n], recv_sem=pr.at[j, n],
            device_id=(2 * z + 1 - core, h), device_id_type=MESH,
        )

    def z_own(j):
        for unit in range(2):
            for way in range(2):
                z_copy(j, 0, unit, way, z).start()
        p_copy(j, 0, z, core).start()

    def tick(j, t):
        left, right = along(-1 - t), lax.rem(z + 1 + t, 8)
        for unit in range(2):
            for way in range(2):
                at = (left, right)[way]

                def step(last):
                    z_copy(j, t, unit, way, at).wait_recv()

                    @pl.when(t < last)
                    def _():
                        z_copy(j, t + 1, unit, way, at).start()

                if unit == way:
                    step(3)
                else:
                    pl.when(t < 3)(functools.partial(step, 2))
        p_copy(j, 1 + 2 * t, left, core).start()

        @pl.when(t < 3)
        def _():
            p_copy(j, 2 + 2 * t, right, core).start()

        if j < 4:

            @pl.when(t == 2)
            def _():
                z_own(j + 1)

    def p_wait(j):
        p_copy(j, 0, z, 1 - core).wait_recv()

        @pl.loop(0, 4)
        def _(t):
            p_copy(j, 1 + 2 * t, along(-1 - t), 1 - core).wait_recv()

            @pl.when(t < 3)
            def _():
                p_copy(j, 2 + 2 * t, lax.rem(z + 1 + t, 8), 1 - core).wait_recv()

    ORDER = (2, 3, 1, 0, 4)

    for k in range(1, 16):
        w1(k, lax.rem(h - k + 16, 16)).wait_recv()
    for j in range(5):
        piece = wraw[:, :, pl.ds(ORDER[j] * part, part)]
        wfull[j, slab(z, core), :] = piece.reshape(64, part)
    z_own(0)

    def projected(j, t):
        at = pl.ds(pl.multiple_of(t * 256, 256), 256)
        return at, silu(jnp.dot(normed[at, :], wfull[j], preferred_element_type=jnp.float32))

    def tile_q(t):
        _, v = projected(0, t)
        v = v.astype(jnp.bfloat16)
        for c in range(CHUNKS):
            for k in range(2):
                q[c, 2 * t + k] = v[k * rows : (k + 1) * rows, c * cols : (c + 1) * cols]

    def tile_k(t):
        at, v = projected(1, t)
        for c in range(CHUNKS):
            mine = jnp.concatenate([q[c, 2 * t], q[c, 2 * t + 1]], axis=0).astype(jnp.float32)
            for k in range(cols // 128):
                head = slice(c * cols + k * 128, c * cols + (k + 1) * 128)
                dots = jnp.sum(mine[:, k * 128 : (k + 1) * 128] * v[:, head], axis=-1, keepdims=True)
                own[at, head] = jnp.broadcast_to(silu(alpha * dots), (256, 128))

    def tile_v(t):
        at, v = projected(2, t)
        own[at, :] = own[at, :] * v

    def tile_u(t):
        at, v = projected(3, t)
        gate[at, :] = v

    def q_copy(c, k):
        way, held = GROUPS[k]
        span = pl.ds(STARTS[k], len(held))
        return pltpu.make_async_remote_copy(
            src_ref=qs.at[c, span], dst_ref=qr.at[c, span], send_sem=qss.at[c, k], recv_sem=qrs.at[c, k],
            device_id=(g, plane(turn(way, c))), device_id_type=MESH,
        )

    def r_copy(c, k):
        way, held = GROUPS[k]
        dy, dx = turn(way, c)
        return pltpu.make_async_remote_copy(
            src_ref=res.at[c, pl.ds(STARTS[k], len(held))],
            dst_ref=mix.at[c, pl.ds(HERE + STARTS[k], len(held))],
            send_sem=rss.at[c, k], recv_sem=rrs.at[c, k],
            device_id=(g, plane((-dy, -dx))), device_id_type=MESH,
        )

    def ask():
        @pl.loop(0, CHUNKS)
        def _(c):
            for k, (_, held) in enumerate(GROUPS):
                for n in range(len(held)):
                    at = STARTS[k] + n
                    qs[c, at] = q[c, block_of[user_of(c, HERE + at)]]
            for k in range(len(GROUPS)):
                q_copy(c, k).start()

    def attend(c):
        for k in range(len(GROUPS)):
            q_copy(c, k).wait_recv()
        for held in range(HERE):
            from_here = q[c, block_of[user_of(c, held)]]
            others = [p for p, (_, at) in enumerate(SENT) if at == held]
            rows_in = jnp.concatenate([from_here] + [qr[c, p] for p in others], axis=0)
            for k in range(cols // 128):
                head = slice(k * 128, (k + 1) * 128)
                raw = lax.dot_general(
                    rows_in[:, head], kv[c, held, 0:256, head], (((1,), (1,)), ((), ())),
                    preferred_element_type=jnp.float32,
                )
                weight = silu(alpha * raw).astype(jnp.bfloat16)
                out = jnp.dot(weight, kv[c, held, 256:512, head], preferred_element_type=jnp.float32)
                out = out.astype(jnp.bfloat16)
                mix[c, held, :, head] = out[0:rows]
                for n, p in enumerate(others):
                    res[c, p, :, head] = out[(n + 1) * rows : (n + 2) * rows]
        for k in range(len(GROUPS)):
            r_copy(c, k).start()

    def leaves(c):
        for child in range(1, HERE):
            if child not in PARENT:
                kv_send(c, child).wait_recv()

    tiles = (None, tile_q, tile_k, tile_v, tile_u)
    for j in range(5):

        @pl.loop(0, 4)
        def _(t):
            tick(j, t)
            if tiles[j] is not None:
                tiles[j](t)

        p_wait(j)
        if j == 0:
            kv_level(1, None)
        if j == 1:
            ask()
            kv_level(2, None)
        if j == 2:
            for c in range(CHUNKS):
                leaves(c)
            pl.loop(0, 2)(attend)
        if j == 3:
            pl.loop(2, 4)(attend)

    for c in range(CHUNKS):
        for k in range(len(GROUPS)):
            r_copy(c, k).wait_recv()

    one = lax.broadcasted_iota(jnp.int32, (rows, rows), 0) == lax.broadcasted_iota(jnp.int32, (rows, rows), 1)
    lane = lax.broadcasted_iota(jnp.int32, (1, rows), 1)

    @pl.loop(0, blocks // 2)
    def _(t):
        pair = []
        for k in range(2):
            b = 2 * t + k
            at = pl.ds(pl.multiple_of(b * rows, rows), rows)
            prefix = jnp.concatenate(
                [mix[c, place_of[c * 16 + users[b]]] for c in range(CHUNKS)], axis=1
            ).astype(jnp.float32)
            v = centred(prefix + own[at, :]) * gain_mid[...] * gate[at, :]
            pair.append(v.astype(jnp.bfloat16))
        gated = jnp.concatenate(pair, axis=0)
        out = jnp.dot(gated, wfull[4], preferred_element_type=jnp.float32)
        for k in range(2):
            b = 2 * t + k
            v = xb[b].astype(jnp.float32) + out[k * rows : (k + 1) * rows]
            emb[b] = v.astype(jnp.bfloat16)
            line = jnp.sum(centred(v) * score_vec[...], axis=-1, keepdims=True)
            line = jnp.sum(jnp.where(one, jnp.broadcast_to(line, (rows, rows)), 0.0), axis=0, keepdims=True)
            scores[pl.ds(b, 1), :] = jnp.where(lane < live[b], line, 0.0)

    for copy in sent:
        copy.wait_send()
    for j in range(5):
        for unit in range(2):
            for way in range(2):
                for t in range(4 if unit == way else 3):
                    z_copy(j, t, unit, way, z).wait_send()
        for n in range(8):
            p_copy(j, n, z, core).wait_send()
    for c in range(CHUNKS):
        for k in range(len(GROUPS)):
            q_copy(c, k).wait_send()
            r_copy(c, k).wait_send()


def shards(
    candidates, block_user, live_rows, prefix_keys, prefix_values, w_proj, w_out, gain_in, gain_mid, score_vec
):
    blocks, rows, width = candidates.shape
    dma = pltpu.SemaphoreType.DMA
    bf, f32 = jnp.bfloat16, jnp.float32
    cols = width // CHUNKS
    others, groups = len(SENT), len(GROUPS)
    vmem = pl.BlockSpec(memory_space=pltpu.VMEM)
    smem = pl.BlockSpec(memory_space=pltpu.SMEM)
    anywhere = pl.BlockSpec(memory_space=pl.ANY)
    return pl.pallas_call(
        kernel,
        out_shape=(
            jax.ShapeDtypeStruct((blocks, rows, width), bf),
            jax.ShapeDtypeStruct((blocks, rows), f32),
        ),
        in_specs=[anywhere, smem, smem, anywhere, anywhere, anywhere, anywhere, vmem, vmem, vmem],
        out_specs=(vmem, vmem),
        scratch_shapes=[
            pltpu.VMEM((blocks, rows, width), bf),
            pltpu.VMEM((blocks * rows, width), bf),
            pltpu.VMEM((16, 4, 5 * width), bf),
            pltpu.VMEM((5, width, width), bf),
            pltpu.VMEM((CHUNKS, HERE, 512, cols), bf),
            pltpu.VMEM((CHUNKS, blocks, rows, cols), bf),
            pltpu.VMEM((blocks * rows, width), f32),
            pltpu.VMEM((blocks * rows, width), f32),
            pltpu.VMEM((CHUNKS, others, rows, cols), bf),
            pltpu.VMEM((CHUNKS, others, rows, cols), bf),
            pltpu.VMEM((CHUNKS, others, rows, cols), bf),
            pltpu.VMEM((CHUNKS, PAIRS, rows, cols), bf),
            pltpu.SMEM((16,), jnp.int32),
            pltpu.SMEM((CHUNKS * 16,), jnp.int32),
            dma((11,)),
            dma((16,)), dma((16,)),
            dma((5, 16)), dma((5, 16)),
            dma((5, 8)), dma((5, 8)),
            dma((CHUNKS, HERE)), dma((CHUNKS, HERE)),
            dma((CHUNKS, groups)), dma((CHUNKS, groups)),
            dma((CHUNKS, groups)), dma((CHUNKS, groups)),
        ],
        compiler_params=pltpu.CompilerParams(
            collective_id=0, has_side_effects=True, vmem_limit_bytes=62 * 1024 * 1024
        ),
    )(
        candidates, block_user, live_rows, prefix_keys, prefix_values, w_proj, w_out,
        gain_in[None, :], gain_mid[None, :], score_vec[None, :],
    )


def solution(mesh):
    placed = (
        P(("group", "helper"), None, None),
        P(("group", "helper")),
        P(("group", "helper")),
        P(("group", "helper"), None, None),
        P(("group", "helper"), None, None),
        P(("group", "helper"), None),
        P(("group", "helper"), None),
        P(),
        P(),
        P(),
    )
    return jax.shard_map(
        shards,
        mesh=mesh,
        in_specs=placed,
        out_specs=(P(("group", "helper"), None, None), P(("group", "helper"), None)),
        check_vma=False,
    )
```

time: 308 us -> 126 us (0.41)
  waiting for transfers between devices: 135 us -> 0 us
  Pallas kernels: 0 us -> 122 us
  local copies, waits for them, and re-layouts: 59.7 us -> 3.68 us
  matrix products: 31.6 us -> 0 us
  starting transfers between devices: 22.4 us -> 0 us
  other arithmetic: 22.1 us -> 0 us
  blocking collectives: 20.1 us -> 0 us
  between operations: 14.3 us -> 0.65 us
    pallas_call x0 -> x1, Pallas kernels: none -> 122 us  [shards(): pl.pallas_call(kernel, out_shape=(jax.ShapeDtypeStruct((blocks, rows, wid...]
    all_gather x1 -> x0, waiting for transfers between devices: 67.6 us -> none  [side_by_side(): filled = lax.all_gather(both, axis, axis=dim, tiled=True)]
    all_to_all x4 -> x0, waiting for transfers between devices: 67.2 us -> none  [the longest x2 42 us: exchange_in_groups(): lax.all_to_all(group, axis, split_axis=split_dim, concat_axis=concat_dim,...]
    dot_general x8 -> x0, matrix products: 31.6 us -> none  [the longest x1 13.2 us: shards(): jnp.dot(normed, proj_full, preferred_element_type=jnp.float32)]
    all_to_all x4 -> x0, starting transfers between devices: 22.3 us -> none  [the longest x2 11.2 us: attend(): lax.all_to_all(mixed_heads.reshape(arrived_shape), 'helper', split_axis=0...]
    all_gather x1 -> x0, blocking collectives: 20.1 us -> none  [side_by_side(): filled = lax.all_gather(both, axis, axis=dim, tiled=True)]
    unnamed x34 -> x4, local copies, waits for them, and re-layouts: 23.6 us -> 3.68 us
    reshape x4 -> x0, local copies, waits for them, and re-layouts: 15.7 us -> none  [the longest x2 8.49 us: attend(): mixed_heads.reshape(arrived_shape)]
  transfers between devices with their start and end apart: 5 -> 0, of which waited for: 5 -> 0; matrix products, arithmetic and copies ran while one was open for 18% -> 0% of each run, Pallas kernels for 0% -> 0%
where the time goes in v1:
time: 126 us
  Pallas kernels  122 us (97%)
  local copies, waits for them, and re-layouts  3.68 us (3%)
    pallas_call x1, Pallas kernels, shards(): pl.pallas_call(kernel, out_shape=(jax.ShapeDtypeStruct((blocks, rows, wid...  122 us
    unnamed x4, local copies, waits for them, and re-layouts  3.68 us

profile of v1, /device:TPU:1, one launch (start us, length us, event | category | flops | bytes accessed | tf_op | source)
XLA Modules:
  0.0 125.8 jit_solution(12043277477081727046)
XLA Ops:
  0.6 121.5 %shard_map.113 = (bf16[8,128,1024]{2,1,0:T(8,128)(2,1)}, f32[8,128]{1,0:T(8,128)}) custom-call(bf16[8,128,1024]{2,1,0:T(8,128)(2,1)} %cand.1, s32[8]{0:T(128)} %users.1, s32[8]{0:T(128)} %live.1, bf16[1,256,1024]{2,1,0:T(8,128)(2,1)} %keys.1, bf16[1,256,1024]{2,1,0:T(8,128)(2,1)} %values.1, bf16[4,4096]{1,0:T(4,128)(2,1)} %w_proj.1, bf16[4,1024]{1,0:T(4,128)(2,1)} %w_out.1, ...), custom_call_target="tpu_custom_call" | custom-call | tf_op jit(solution)/shard_map/pallas_call | solution.py:405
  122.2 0.0 copy-start
  122.2 3.1 %copy.14 = bf16[8,128,1024]{2,1,0:T(8,128)(2,1)} copy(bf16[8,128,1024]{2,1,0:T(8,128)(2,1)} %get-tuple-element.4) | data formatting | bytes 4194304
  125.3 0.0 copy-done
  125.3 0.6 copy.15
Async XLA Ops:
  122.2 3.1 %copy-start = (f32[8,128]{1,0:T(8,128)S(1)}, f32[8,128]{1,0:T(8,128)}, u32[]{:S(2)}) copy-start(f32[8,128]{1,0:T(8,128)} %get-tuple-element.5) | copy-start | bytes 12292

commit v2 on v1

--- a/solution.py
+++ b/solution.py
@@ -35,6 +35,7 @@
 STARTS = tuple(sum(len(h) for _, h in GROUPS[:k]) for k in range(len(GROUPS)))
 SENT = tuple((way, held) for way, helds in GROUPS for held in helds)
 HERE = len(HOLD)
+UNITS = 2
 PAIRS = HERE + len(SENT)
 
 
@@ -55,9 +56,9 @@
 
 
 def kernel(
-    cand, users, live, keys, values, w_proj, w_out, gain_in, gain_mid, score_vec,
+    cand, users, live, keys, values, w_proj, w_out, gain_in_hbm, gain_mid_hbm, score_vec_hbm,
     emb, scores,
-    xb, normed, wraw, wfull, kv, q, own, gate, qs, qr, res, mix, block_of, place_of,
+    xb, normed, wraw, wfull, kv, q, own, gate, qs, qr, res, mix, gain_in, gain_mid, score_vec, block_of, place_of,
     loc, w1s, w1r, zs, zr, ps, pr, ks, kr, qss, qrs, rss, rrs,
 ):
     g, h = lax.axis_index("group"), lax.axis_index("helper")
@@ -75,8 +76,13 @@
         return lax.rem(z + step + 8, 8)
 
     local = [
-        pltpu.make_async_copy(w_proj, wraw.at[h, :, pl.ds(0, 4 * part)], loc.at[0]),
-        pltpu.make_async_copy(w_out, wraw.at[h, :, pl.ds(4 * part, part)], loc.at[1]),
+        pltpu.make_async_copy(
+            w_proj.at[:, pl.ds(2 * part, 2 * part)], wraw.at[h, :, pl.ds(0, 2 * part)], loc.at[0]
+        ),
+        pltpu.make_async_copy(
+            w_proj.at[:, pl.ds(0, 2 * part)], wraw.at[h, :, pl.ds(2 * part, 2 * part)], loc.at[1]
+        ),
+        pltpu.make_async_copy(w_out, wraw.at[h, :, pl.ds(4 * part, part)], loc.at[11]),
         pltpu.make_async_copy(cand, xb, loc.at[2]),
     ]
     for c in range(CHUNKS):
@@ -88,6 +94,8 @@
                     loc.at[3 + 2 * c + k],
                 )
             )
+    for k, (src, dst) in enumerate(((gain_in_hbm, gain_in), (gain_mid_hbm, gain_mid), (score_vec_hbm, score_vec))):
+        local.append(pltpu.make_async_copy(src, dst, loc.at[12 + k]))
     for copy in local:
         copy.start()
 
@@ -107,19 +115,21 @@
         copy.start()
         return copy
 
-    local[0].wait()
-    local[1].wait()
-
-    def w1(k, at):
-        return pltpu.make_async_remote_copy(
-            src_ref=wraw.at[at], dst_ref=wraw.at[at], send_sem=w1s.at[k], recv_sem=w1r.at[k],
+    for copy in local[:3]:
+        copy.wait()
+
+    def w1(n, k, at):
+        ref = wraw.at[at, :, pl.ds(*((0, part), (part, 4 * part))[n])]
+        return pltpu.make_async_remote_copy(
+            src_ref=ref, dst_ref=ref, send_sem=w1s.at[n, k], recv_sem=w1r.at[n, k],
             device_id=(g, lax.rem(h + k, 16)), device_id_type=MESH,
         )
 
-    for k in range(1, 16):
-        copy = w1(k, h)
-        copy.start()
-        sent.append(copy)
+    for n in range(2):
+        for k in range(1, 16):
+            copy = w1(n, k, h)
+            copy.start()
+            sent.append(copy)
 
     def kv_send(c, child):
         parent = PARENT[child]
@@ -131,11 +141,11 @@
             recv_sem=kr.at[c, child], device_id=(g, plane(step)), device_id_type=MESH,
         )
 
-    def kv_level(level, after):
+    def kv_level(level):
         for c in range(CHUNKS):
             if level == 0:
-                local[3 + 2 * c].wait()
                 local[4 + 2 * c].wait()
+                local[5 + 2 * c].wait()
             for child in LEVELS[level]:
                 if PARENT[child]:
                     kv_send(c, PARENT[child]).wait_recv()
@@ -143,7 +153,7 @@
                 copy.start()
                 sent.append(copy)
 
-    kv_level(0, None)
+    kv_level(0)
 
     for u in range(16):
         found = jnp.int32(0)
@@ -163,7 +173,8 @@
         for p in range(PAIRS):
             place_of[c * 16 + user_of(c, p)] = jnp.int32(p)
 
-    local[2].wait()
+    for k in (3, 12, 13, 14):
+        local[k].wait()
 
     @pl.loop(0, blocks)
     def _(b):
@@ -174,8 +185,8 @@
         return pl.ds(pl.multiple_of((2 * at + of_core) * 64, 64), 64)
 
     def z_copy(j, t, unit, way, at):
-        ref = wfull.at[j, slab(at, core), pl.ds(unit * (part // 2), part // 2)]
-        where = (t * 2 + unit) * 2 + way
+        ref = wfull.at[j, slab(at, core), pl.ds(unit * (part // UNITS), part // UNITS)]
+        where = (t * UNITS + unit) * 2 + way
         return pltpu.make_async_remote_copy(
             src_ref=ref, dst_ref=ref, send_sem=zs.at[j, where], recv_sem=zr.at[j, where],
             device_id=(2 * along(1 - 2 * way) + core, h), device_id_type=MESH,
@@ -189,14 +200,14 @@
         )
 
     def z_own(j):
-        for unit in range(2):
+        for unit in range(UNITS):
             for way in range(2):
                 z_copy(j, 0, unit, way, z).start()
         p_copy(j, 0, z, core).start()
 
     def tick(j, t):
         left, right = along(-1 - t), lax.rem(z + 1 + t, 8)
-        for unit in range(2):
+        for unit in range(UNITS):
             for way in range(2):
                 at = (left, right)[way]
 
@@ -207,7 +218,7 @@
                     def _():
                         z_copy(j, t + 1, unit, way, at).start()
 
-                if unit == way:
+                if unit % 2 == way:
                     step(3)
                 else:
                     pl.when(t < 3)(functools.partial(step, 2))
@@ -217,12 +228,6 @@
         def _():
             p_copy(j, 2 + 2 * t, right, core).start()
 
-        if j < 4:
-
-            @pl.when(t == 2)
-            def _():
-                z_own(j + 1)
-
     def p_wait(j):
         p_copy(j, 0, z, 1 - core).wait_recv()
 
@@ -234,13 +239,16 @@
             def _():
                 p_copy(j, 2 + 2 * t, lax.rem(z + 1 + t, 8), 1 - core).wait_recv()
 
-    ORDER = (2, 3, 1, 0, 4)
-
-    for k in range(1, 16):
-        w1(k, lax.rem(h - k + 16, 16)).wait_recv()
-    for j in range(5):
-        piece = wraw[:, :, pl.ds(ORDER[j] * part, part)]
-        wfull[j, slab(z, core), :] = piece.reshape(64, part)
+    STANDS = (0, 1, 3, 2, 4)
+
+    def stage_one(n):
+        for k in range(1, 16):
+            w1(n, k, lax.rem(h - k + 16, 16)).wait_recv()
+        for j in ((0,), (1, 2, 3, 4))[n]:
+            piece = wraw[:, :, pl.ds(STANDS[j] * part, part)]
+            wfull[j, slab(z, core), :] = piece.reshape(64, part)
+
+    stage_one(0)
     z_own(0)
 
     def projected(j, t):
@@ -326,27 +334,45 @@
             if child not in PARENT:
                 kv_send(c, child).wait_recv()
 
-    tiles = (None, tile_q, tile_k, tile_v, tile_u)
-    for j in range(5):
-
-        @pl.loop(0, 4)
-        def _(t):
-            tick(j, t)
-            if tiles[j] is not None:
-                tiles[j](t)
-
-        p_wait(j)
+    tiles = (None, tile_k, tile_v, tile_u)
+    for j in range(6):
+
+        def step(half):
+            if j > 0:
+                tick(j - 1, 2 + half)
+            if j < 5:
+                tick(j, half)
+            if 0 < j < 4:
+
+                @pl.when(half == 0)
+                def _():
+                    z_own(j + 1)
+
+            if j > 2:
+                pl.loop(2 * half, 2 * half + 2)(tiles[j - 2])
+            if j in (3, 4):
+                attend(2 * (j - 3) + half)
+
         if j == 0:
-            kv_level(1, None)
+            step(0)
+            stage_one(1)
+            z_own(1)
+            step(1)
+            continue
         if j == 1:
+            step(0)
+            kv_level(1)
+            step(1)
+            p_wait(0)
+            pl.loop(0, 4)(tile_q)
+            kv_level(2)
             ask()
-            kv_level(2, None)
+            continue
+        pl.loop(0, 2)(step)
+        p_wait(j - 1)
         if j == 2:
             for c in range(CHUNKS):
                 leaves(c)
-            pl.loop(0, 2)(attend)
-        if j == 3:
-            pl.loop(2, 4)(attend)
 
     for c in range(CHUNKS):
         for k in range(len(GROUPS)):
@@ -379,9 +405,9 @@
     for copy in sent:
         copy.wait_send()
     for j in range(5):
-        for unit in range(2):
+        for unit in range(UNITS):
             for way in range(2):
-                for t in range(4 if unit == way else 3):
+                for t in range(4 if unit % 2 == way else 3):
                     z_copy(j, t, unit, way, z).wait_send()
         for n in range(8):
             p_copy(j, n, z, core).wait_send()
@@ -401,6 +427,7 @@
     others, groups = len(SENT), len(GROUPS)
     vmem = pl.BlockSpec(memory_space=pltpu.VMEM)
     smem = pl.BlockSpec(memory_space=pltpu.SMEM)
+    stay = functools.partial(pltpu.with_memory_space_constraint, memory_space=pltpu.HBM)
     anywhere = pl.BlockSpec(memory_space=pl.ANY)
     return pl.pallas_call(
         kernel,
@@ -408,7 +435,7 @@
             jax.ShapeDtypeStruct((blocks, rows, width), bf),
             jax.ShapeDtypeStruct((blocks, rows), f32),
         ),
-        in_specs=[anywhere, smem, smem, anywhere, anywhere, anywhere, anywhere, vmem, vmem, vmem],
+        in_specs=[anywhere, smem, smem] + [anywhere] * 7,
         out_specs=(vmem, vmem),
         scratch_shapes=[
             pltpu.VMEM((blocks, rows, width), bf),
@@ -423,22 +450,25 @@
             pltpu.VMEM((CHUNKS, others, rows, cols), bf),
             pltpu.VMEM((CHUNKS, others, rows, cols), bf),
             pltpu.VMEM((CHUNKS, PAIRS, rows, cols), bf),
+            pltpu.VMEM((1, width), f32),
+            pltpu.VMEM((1, width), f32),
+            pltpu.VMEM((1, width), f32),
             pltpu.SMEM((16,), jnp.int32),
             pltpu.SMEM((CHUNKS * 16,), jnp.int32),
-            dma((11,)),
-            dma((16,)), dma((16,)),
-            dma((5, 16)), dma((5, 16)),
+            dma((15,)),
+            dma((2, 16)), dma((2, 16)),
+            dma((5, 8 * UNITS)), dma((5, 8 * UNITS)),
             dma((5, 8)), dma((5, 8)),
             dma((CHUNKS, HERE)), dma((CHUNKS, HERE)),
             dma((CHUNKS, groups)), dma((CHUNKS, groups)),
             dma((CHUNKS, groups)), dma((CHUNKS, groups)),
         ],
         compiler_params=pltpu.CompilerParams(
-            collective_id=0, has_side_effects=True, vmem_limit_bytes=62 * 1024 * 1024
+            collective_id=0, has_side_effects=True, vmem_limit_bytes=48 * 1024 * 1024
         ),
     )(
-        candidates, block_user, live_rows, prefix_keys, prefix_values, w_proj, w_out,
-        gain_in[None, :], gain_mid[None, :], score_vec[None, :],
+        stay(candidates), stay(block_user), stay(live_rows), stay(prefix_keys), stay(prefix_values), stay(w_proj), stay(w_out),
+        stay(gain_in[None, :]), stay(gain_mid[None, :]), stay(score_vec[None, :]),
     )
 
 

time: 126 us -> 94.4 us (0.75)
  Pallas kernels: 122 us -> 91.8 us
  local copies, waits for them, and re-layouts: 3.68 us -> 1.91 us
    pallas_call x1, Pallas kernels: 122 us -> 91.8 us  [shards(): pl.pallas_call(kernel, out_shape=(jax.ShapeDtypeStruct((blocks, rows, wid...]
    unnamed x4 -> x2, local copies, waits for them, and re-layouts: 3.68 us -> 1.91 us
where the time goes in v2:
time: 94.4 us; the launch traced here: 94.3 us
  Pallas kernels  91.8 us (97%)
  local copies, waits for them, and re-layouts  1.91 us (2%)
    pallas_call x1, Pallas kernels, shards(): pl.pallas_call(kernel, out_shape=(jax.ShapeDtypeStruct((blocks, rows, wid...  91.8 us
    unnamed x2, local copies, waits for them, and re-layouts  1.91 us

profile of v2, /device:TPU:1, one launch (start us, length us, event | category | flops | bytes accessed | tf_op | source)
XLA Modules:
  0.0 94.3 jit_solution(3537041210065726027)
XLA Ops:
  0.6 91.8 %shard_map.113 = (bf16[8,128,1024]{2,1,0:T(8,128)(2,1)S(1)}, f32[8,128]{1,0:T(8,128)S(1)}) custom-call(bf16[8,128,1024]{2,1,0:T(8,128)(2,1)} %cand.1, s32[8]{0:T(128)} %users.1, s32[8]{0:T(128)} %live.1, bf16[1,256,1024]{2,1,0:T(8,128)(2,1)} %keys.1, bf16[1,256,1024]{2,1,0:T(8,128)(2,1)} %values.1, bf16[4,4096]{1,0:T(4,128)(2,1)} %w_proj.1, ...), custom_call_target="tpu_custom_call" | custom-call | tf_op jit(solution)/shard_map/pallas_call | solution.py:432
  92.4 1.3 %copy.14 = bf16[8,128,1024]{2,1,0:T(8,128)(2,1)} copy(bf16[8,128,1024]{2,1,0:T(8,128)(2,1)S(1)} %get-tuple-element.4) | data formatting | bytes 4194304
  93.7 0.6 copy.15

commit v3 on v2

--- a/solution.py
+++ b/solution.py
@@ -35,6 +35,8 @@
 STARTS = tuple(sum(len(h) for _, h in GROUPS[:k]) for k in range(len(GROUPS)))
 SENT = tuple((way, held) for way, helds in GROUPS for held in helds)
 HERE = len(HOLD)
+FIRST, SECOND = (0, 2), (1, 3)
+STARTS_AT = (0, 1, 3, 4, 6)
 UNITS = 2
 PAIRS = HERE + len(SENT)
 
@@ -141,8 +143,8 @@
             recv_sem=kr.at[c, child], device_id=(g, plane(step)), device_id_type=MESH,
         )
 
-    def kv_level(level):
-        for c in range(CHUNKS):
+    def kv_level(level, chunks):
+        for c in chunks:
             if level == 0:
                 local[4 + 2 * c].wait()
                 local[5 + 2 * c].wait()
@@ -153,7 +155,7 @@
                 copy.start()
                 sent.append(copy)
 
-    kv_level(0)
+    kv_level(0, FIRST + SECOND)
 
     for u in range(16):
         found = jnp.int32(0)
@@ -297,12 +299,13 @@
             device_id=(g, plane((-dy, -dx))), device_id_type=MESH,
         )
 
-    def ask():
-        @pl.loop(0, CHUNKS)
-        def _(c):
+    def ask(chunks):
+        @pl.loop(0, len(chunks))
+        def _(n):
+            c = chunks[0] + 2 * n
             for k, (_, held) in enumerate(GROUPS):
-                for n in range(len(held)):
-                    at = STARTS[k] + n
+                for m in range(len(held)):
+                    at = STARTS[k] + m
                     qs[c, at] = q[c, block_of[user_of(c, HERE + at)]]
             for k in range(len(GROUPS)):
                 q_copy(c, k).start()
@@ -334,45 +337,45 @@
             if child not in PARENT:
                 kv_send(c, child).wait_recv()
 
-    tiles = (None, tile_k, tile_v, tile_u)
-    for j in range(6):
-
-        def step(half):
-            if j > 0:
-                tick(j - 1, 2 + half)
-            if j < 5:
-                tick(j, half)
-            if 0 < j < 4:
-
-                @pl.when(half == 0)
-                def _():
-                    z_own(j + 1)
-
-            if j > 2:
-                pl.loop(2 * half, 2 * half + 2)(tiles[j - 2])
-            if j in (3, 4):
-                attend(2 * (j - 3) + half)
-
-        if j == 0:
-            step(0)
+    def some(work, a, b):
+        return lambda: pl.loop(a, b)(work)
+
+    def half(level, chunks):
+        return lambda: kv_level(level, chunks)
+
+    def answer(chunks):
+        def work():
+            for c in chunks:
+                leaves(c)
+            pl.loop(0, len(chunks))(lambda n: attend(chunks[0] + 2 * n))
+
+        return work
+
+    after = {
+        1: (half(1, FIRST),),
+        2: (half(1, SECOND),),
+        3: (half(2, FIRST), some(tile_q, 0, 4), lambda: ask(FIRST)),
+        4: (half(2, SECOND), lambda: ask(SECOND), some(tile_k, 0, 2)),
+        5: (some(tile_k, 2, 4),),
+        6: (answer(FIRST), some(tile_v, 0, 2)),
+        7: (answer(SECOND), some(tile_v, 2, 4)),
+        8: (some(tile_u, 0, 2),),
+        9: (some(tile_u, 2, 4),),
+    }
+    for s in range(STARTS_AT[-1] + 4):
+        for j, start in enumerate(STARTS_AT):
+            if 0 <= s - start < 4:
+                tick(j, s - start)
+        if s == 0:
             stage_one(1)
-            z_own(1)
-            step(1)
-            continue
-        if j == 1:
-            step(0)
-            kv_level(1)
-            step(1)
-            p_wait(0)
-            pl.loop(0, 4)(tile_q)
-            kv_level(2)
-            ask()
-            continue
-        pl.loop(0, 2)(step)
-        p_wait(j - 1)
-        if j == 2:
-            for c in range(CHUNKS):
-                leaves(c)
+        for j, start in enumerate(STARTS_AT):
+            if start == s + 1:
+                z_own(j)
+        for j, start in enumerate(STARTS_AT):
+            if start + 3 == s:
+                p_wait(j)
+        for work in after.get(s, ()):
+            work()
 
     for c in range(CHUNKS):
         for k in range(len(GROUPS)):
@@ -381,19 +384,20 @@
     one = lax.broadcasted_iota(jnp.int32, (rows, rows), 0) == lax.broadcasted_iota(jnp.int32, (rows, rows), 1)
     lane = lax.broadcasted_iota(jnp.int32, (1, rows), 1)
 
-    @pl.loop(0, blocks // 2)
-    def _(t):
-        pair = []
+    def before(t):
         for k in range(2):
             b = 2 * t + k
-            at = pl.ds(pl.multiple_of(b * rows, rows), rows)
+            at = pl.ds(b * rows, rows)
             prefix = jnp.concatenate(
                 [mix[c, place_of[c * 16 + users[b]]] for c in range(CHUNKS)], axis=1
             ).astype(jnp.float32)
             v = centred(prefix + own[at, :]) * gain_mid[...] * gate[at, :]
-            pair.append(v.astype(jnp.bfloat16))
-        gated = jnp.concatenate(pair, axis=0)
-        out = jnp.dot(gated, wfull[4], preferred_element_type=jnp.float32)
+            normed[at, :] = v.astype(jnp.bfloat16)
+
+    def product(t):
+        return jnp.dot(normed[pl.ds(t * 256, 256), :], wfull[4], preferred_element_type=jnp.float32)
+
+    def after_product(t, out):
         for k in range(2):
             b = 2 * t + k
             v = xb[b].astype(jnp.float32) + out[k * rows : (k + 1) * rows]
@@ -401,6 +405,13 @@
             line = jnp.sum(centred(v) * score_vec[...], axis=-1, keepdims=True)
             line = jnp.sum(jnp.where(one, jnp.broadcast_to(line, (rows, rows)), 0.0), axis=0, keepdims=True)
             scores[pl.ds(b, 1), :] = jnp.where(lane < live[b], line, 0.0)
+
+    before(0)
+    for t in range(blocks // 2):
+        out = product(t)
+        if t + 1 < blocks // 2:
+            before(t + 1)
+        after_product(t, out)
 
     for copy in sent:
         copy.wait_send()

time: 94.4 us -> 90.7 us (0.961)
  Pallas kernels: 91.8 us -> 88.1 us
    pallas_call x1, Pallas kernels: 91.8 us -> 88.1 us  [shards(): pl.pallas_call(kernel, out_shape=(jax.ShapeDtypeStruct((blocks, rows, wid...]
where the time goes in v3:
time: 90.7 us; the launch traced here: 90.6 us
  Pallas kernels  88.1 us (97%)
  local copies, waits for them, and re-layouts  1.91 us (2%)
    pallas_call x1, Pallas kernels, shards(): pl.pallas_call(kernel, out_shape=(jax.ShapeDtypeStruct((blocks, rows, wid...  88.1 us
    unnamed x2, local copies, waits for them, and re-layouts  1.91 us

profile of v3, /device:TPU:1, one launch (start us, length us, event | category | flops | bytes accessed | tf_op | source)
XLA Modules:
  0.0 90.6 jit_solution(7852318063030282282)
XLA Ops:
  0.6 88.1 %shard_map.113 = (bf16[8,128,1024]{2,1,0:T(8,128)(2,1)S(1)}, f32[8,128]{1,0:T(8,128)S(1)}) custom-call(bf16[8,128,1024]{2,1,0:T(8,128)(2,1)} %cand.1, s32[8]{0:T(128)} %users.1, s32[8]{0:T(128)} %live.1, bf16[1,256,1024]{2,1,0:T(8,128)(2,1)} %keys.1, bf16[1,256,1024]{2,1,0:T(8,128)(2,1)} %values.1, bf16[4,4096]{1,0:T(4,128)(2,1)} %w_proj.1, ...), custom_call_target="tpu_custom_call" | custom-call | tf_op jit(solution)/shard_map/pallas_call | solution.py:443
  88.7 1.3 %copy.14 = bf16[8,128,1024]{2,1,0:T(8,128)(2,1)} copy(bf16[8,128,1024]{2,1,0:T(8,128)(2,1)S(1)} %get-tuple-element.4) | data formatting | bytes 4194304
  90.1 0.6 copy.15

commit v4 on v3

--- a/solution.py
+++ b/solution.py
@@ -36,7 +36,7 @@
 SENT = tuple((way, held) for way, helds in GROUPS for held in helds)
 HERE = len(HOLD)
 FIRST, SECOND = (0, 2), (1, 3)
-STARTS_AT = (0, 1, 3, 4, 6)
+STARTS_AT = (0, 1, 3, 4, 5)
 UNITS = 2
 PAIRS = HERE + len(SENT)
 
@@ -343,6 +343,9 @@
     def half(level, chunks):
         return lambda: kv_level(level, chunks)
 
+    def whole(j):
+        return lambda: p_wait(j)
+
     def answer(chunks):
         def work():
             for c in chunks:
@@ -354,13 +357,12 @@
     after = {
         1: (half(1, FIRST),),
         2: (half(1, SECOND),),
-        3: (half(2, FIRST), some(tile_q, 0, 4), lambda: ask(FIRST)),
-        4: (half(2, SECOND), lambda: ask(SECOND), some(tile_k, 0, 2)),
-        5: (some(tile_k, 2, 4),),
-        6: (answer(FIRST), some(tile_v, 0, 2)),
-        7: (answer(SECOND), some(tile_v, 2, 4)),
-        8: (some(tile_u, 0, 2),),
-        9: (some(tile_u, 2, 4),),
+        3: (half(2, FIRST), whole(0), some(tile_q, 0, 4), lambda: ask(FIRST)),
+        4: (half(2, SECOND), lambda: ask(SECOND)),
+        5: (whole(1), some(tile_k, 0, 2)),
+        6: (answer(FIRST), some(tile_k, 2, 4)),
+        7: (answer(SECOND), whole(2), some(tile_v, 0, 2)),
+        8: (some(tile_v, 2, 4), whole(3), some(tile_u, 0, 4), whole(4)),
     }
     for s in range(STARTS_AT[-1] + 4):
         for j, start in enumerate(STARTS_AT):
@@ -371,9 +373,6 @@
         for j, start in enumerate(STARTS_AT):
             if start == s + 1:
                 z_own(j)
-        for j, start in enumerate(STARTS_AT):
-            if start + 3 == s:
-                p_wait(j)
         for work in after.get(s, ()):
             work()
 

time: 90.7 us -> 90.2 us (level)
  the two profiles are of different devices: /device:TPU:1 before, /device:TPU:8 now
where the time goes in v4:
time: 90.2 us; the launch traced here: 90.1 us
  Pallas kernels  87.5 us (97%)
  local copies, waits for them, and re-layouts  1.91 us (2%)
    pallas_call x1, Pallas kernels, shards(): pl.pallas_call(kernel, out_shape=(jax.ShapeDtypeStruct((blocks, rows, wid...  87.5 us
    unnamed x2, local copies, waits for them, and re-layouts  1.91 us

profile of v4, /device:TPU:8, one launch (start us, length us, event | category | flops | bytes accessed | tf_op | source)
XLA Modules:
  0.0 90.1 jit_solution(5231221806054094698)
XLA Ops:
  0.6 87.5 %shard_map.113 = (bf16[8,128,1024]{2,1,0:T(8,128)(2,1)S(1)}, f32[8,128]{1,0:T(8,128)S(1)}) custom-call(bf16[8,128,1024]{2,1,0:T(8,128)(2,1)} %cand.1, s32[8]{0:T(128)} %users.1, s32[8]{0:T(128)} %live.1, bf16[1,256,1024]{2,1,0:T(8,128)(2,1)} %keys.1, bf16[1,256,1024]{2,1,0:T(8,128)(2,1)} %values.1, bf16[4,4096]{1,0:T(4,128)(2,1)} %w_proj.1, ...), custom_call_target="tpu_custom_call" | custom-call | tf_op jit(solution)/shard_map/pallas_call | solution.py:442
  88.2 1.3 %copy.14 = bf16[8,128,1024]{2,1,0:T(8,128)(2,1)} copy(bf16[8,128,1024]{2,1,0:T(8,128)(2,1)S(1)} %get-tuple-element.4) | data formatting | bytes 4194304
  89.5 0.6 copy.15
